TPU v7x, 32 devices: a whole 2x2x4 slice. The times are simulated.
32 devices in a mesh: groups: 2 (over y), blk: 4 (over z), oct: 2 (over x), sub: 2 (over core).
Axes of the slice: x: 2, y: 2, z: 4, core: 2. Of those that a mesh axis runs over, the one named last changes fastest.
Arguments:
- positions: float32 [3, 65536], P(None, ('groups', 'blk', 'oct', 'sub')), parts along dimension 1, may hold values from 0 to 320
- polarizability: float32 [65536], P(('groups', 'blk', 'oct', 'sub')), parts along dimension 0, may hold values from 0.5 to 1.5
- permanent_field: float32 [3, 65536], P(None, ('groups', 'blk', 'oct', 'sub')), parts along dimension 1, may hold values from -40 to 40
- group_id: int32 [65536], P(('groups', 'blk', 'oct', 'sub')), parts along dimension 0, may hold values from 0 to 10921, never falling along the last dimension, each value on 1 to 6 neighbouring positions
- pair_mask: int32 [512, 9], P(('groups', 'blk', 'oct', 'sub')), parts along dimension 0, may hold values from 0 to 1, as said below
Outputs:
- dipoles: float32 [3, 65536], P(None, ('groups', 'blk', 'oct', 'sub')), parts along dimension 1
- residual: float32 [3, 65536], P(None, ('groups', 'blk', 'oct', 'sub')), parts along dimension 1
There are 2 independent parts, one for each index of `groups`. A program takes and returns all parts, laid end to end along the dimension named above; each array names one. Nothing has to cross between parts.
Inputs may be any that keep to these rules, and one draw needn't show every extreme that they name: `group_id`: never falls from one atom to the next; each value names 1 to 6 consecutive atoms. pair_mask[b, 4] = 1, and pair_mask[b, 4 + o] = pair_mask[(b + o) mod 256, 4 - o].
All inputs are finite; a program needn't handle non-finite values.
Results may differ from a plain program's by a relative error of at most 0.0003.
Values sent between devices are 32-bit elements; how exact they have to be, the bound alone decides.
No kernel may reach another device: no remote copies, remote signals or barrier semaphores. Data moves between devices by JAX's collectives and lax.ppermute only.
A program may use at most 64 MiB of HBM per device.

v0:
```python
import math
import jax
import jax.numpy as jnp
import numpy as np
from jax import lax
from jax.sharding import PartitionSpec as P

BOXES_DEV = 2
BLOCK = 128
ORDER = 5
NODE_PAD = 128
ITERS = 2
side_length = 32.0
layer_gap = 2.5
thole_damp = 0.39
highest = lax.Precision.HIGHEST


def padded(cells, sides, width):
    for axis, dim in sides:
        count = lax.axis_size(axis)
        head = lax.slice_in_dim(cells, 0, width, axis=dim)
        tail = lax.slice_in_dim(cells, cells.shape[dim] - width, cells.shape[dim], axis=dim)
        cells = jnp.concatenate(
            [
                lax.ppermute(tail, axis, [(i, (i + 1) % count) for i in range(count)]),
                cells,
                lax.ppermute(head, axis, [((i + 1) % count, i) for i in range(count)]),
            ],
            axis=dim,
        )
    return cells


def wrap_image(delta, period):
    return delta - period * jnp.floor(delta / period + 0.5)


def split_size(total, limit):
    best = 1
    for factor in range(1, min(total, limit) + 1):
        if total % factor == 0:
            best = factor
    return best


def near_tiles(target, source, moments, keep_tile, length_z):
    delta_x = wrap_image(target[0][:, :, None] - source[0][:, None, :], side_length)
    delta_y = wrap_image(target[1][:, :, None] - source[1][:, None, :], side_length)
    delta_z = wrap_image(target[2][:, :, None] - source[2][:, None, :], length_z)
    keep = (keep_tile[:, None, None] > 0.5) & (target[4][:, :, None] != source[4][:, None, :])
    dist_sq = jnp.where(keep, delta_x * delta_x + delta_y * delta_y + delta_z * delta_z, 1.0)
    inv_three = lax.rsqrt(dist_sq) / dist_sq
    scaled = (
        thole_damp
        * dist_sq
        * jnp.sqrt(dist_sq)
        * lax.rsqrt(target[3][:, :, None] * source[3][:, None, :])
    )
    lam_three = -jnp.expm1(-scaled)
    lam_five = lam_three - scaled * jnp.exp(-scaled)
    coef_five = jnp.where(keep, 3.0 * lam_five * inv_three / dist_sq, 0.0)
    coef_three = jnp.where(keep, lam_three * inv_three, 0.0)
    along = (
        delta_x * moments[0][:, None, :]
        + delta_y * moments[1][:, None, :]
        + delta_z * moments[2][:, None, :]
    )
    weighted = coef_five * along
    field_x = jnp.sum(weighted * delta_x - coef_three * moments[0][:, None, :], axis=2)
    field_y = jnp.sum(weighted * delta_y - coef_three * moments[1][:, None, :], axis=2)
    field_z = jnp.sum(weighted * delta_z - coef_three * moments[2][:, None, :], axis=2)
    return jnp.stack([field_x, field_y, field_z])


def near_total(static_ext, dipole_ext, mask_rows, length_z, atom_count):
    reach = (mask_rows.shape[1] - 1) // 2
    width = reach * BLOCK
    blocks = atom_count // BLOCK
    target = static_ext[:, width : width + atom_count].reshape(5, blocks, BLOCK)
    total = jnp.zeros((3, blocks, BLOCK), static_ext.dtype)
    for offset in range(-reach, reach + 1):
        begin = (reach + offset) * BLOCK
        source = static_ext[:, begin : begin + atom_count].reshape(5, blocks, BLOCK)
        moments = dipole_ext[:, begin : begin + atom_count].reshape(3, blocks, BLOCK)
        keep_tile = mask_rows[:, reach + offset].astype(static_ext.dtype)
        total = total + near_tiles(target, source, moments, keep_tile, length_z)
    return total.reshape(3, atom_count)


def node_tables():
    count = ORDER
    roots = np.cos((2.0 * np.arange(count) + 1.0) * np.pi / (2.0 * count))
    degree = np.arange(count)
    coeff = (
        2.0 / count * np.cos(np.outer(2.0 * np.arange(count) + 1.0, degree) * np.pi / (2.0 * count))
    )
    coeff = np.where(degree[None, :] == 0, 1.0 / count, coeff)
    index = np.arange(NODE_PAD)
    live = index < count**3
    safe = np.where(live, index, 0)
    first = safe // (count * count)
    second = safe // count % count
    third = safe % count
    levels = np.arange(count)[None, :]
    pick_a = (first[:, None] == levels) * live[:, None] * 1.0
    pick_b = (second[:, None] == levels) * 1.0
    pick_c = (third[:, None] == levels) * 1.0
    node_x = 16.0 * (1.0 + roots[first])
    node_y = 16.0 * (1.0 + roots[second])
    node_t = roots[third]
    tables = [coeff, pick_a, pick_b, pick_c, node_x, node_y, node_t]
    return [jnp.asarray(item, jnp.float32) for item in tables]


def interpolation(coords, box_ids, box_height):
    coeff, pick_a, pick_b, pick_c, node_x, node_y, node_t = node_tables()
    scaled_x = coords[0] / 16.0 - 1.0
    scaled_y = coords[1] / 16.0 - 1.0
    scaled_z = (
        2.0 * (coords[2] - box_ids.astype(coords.dtype)[:, None] * box_height) / box_height - 1.0
    )

    def basis(values, picks):
        terms = [jnp.ones_like(values), values]
        for degree in range(2, ORDER):
            terms.append(2.0 * values * terms[-1] - terms[-2])
        stacked = jnp.stack(terms[:ORDER])
        smooth = jnp.einsum("kn,nba->kba", coeff, stacked, precision=highest)
        return jnp.einsum("pk,kba->pba", picks, smooth, precision=highest)

    return basis(scaled_x, pick_a) * basis(scaled_y, pick_b) * basis(scaled_z, pick_c)


def far_block(target_ids, source_ids, weights, slabs, box_height, length_z):
    coeff, pick_a, pick_b, pick_c, node_x, node_y, node_t = node_tables()
    height_t = (
        target_ids.astype(weights.dtype)[:, None] * box_height
        + 0.5 * box_height * (1.0 + node_t)[None, :]
    )
    height_s = (
        source_ids.astype(weights.dtype)[:, None] * box_height
        + 0.5 * box_height * (1.0 + node_t)[None, :]
    )
    delta_x = wrap_image(node_x[:, None] - node_x[None, :], side_length)[None, :, None, :]
    delta_y = wrap_image(node_y[:, None] - node_y[None, :], side_length)[None, :, None, :]
    delta_z = wrap_image(height_t[:, :, None, None] - height_s[None, None, :, :], length_z)
    apart = jnp.abs(target_ids[:, None] // BOXES_DEV - source_ids[None, :] // BOXES_DEV)
    apart = jnp.minimum(apart, slabs - apart)
    keep = (apart >= 1)[:, None, :, None]
    dist_sq = jnp.where(
        keep,
        delta_x * delta_x + delta_y * delta_y + delta_z * delta_z + box_height * box_height,
        1.0,
    )
    inv_three = lax.rsqrt(dist_sq) / dist_sq
    coef_five = jnp.where(keep, 3.0 * inv_three / dist_sq, 0.0)
    coef_three = jnp.where(keep, inv_three, 0.0)
    weight_x = weights[:, 0, :][None, None]
    weight_y = weights[:, 1, :][None, None]
    weight_z = weights[:, 2, :][None, None]
    weighted = coef_five * (delta_x * weight_x + delta_y * weight_y + delta_z * weight_z)
    field_x = jnp.sum(weighted * delta_x - coef_three * weight_x, axis=(2, 3))
    field_y = jnp.sum(weighted * delta_y - coef_three * weight_y, axis=(2, 3))
    field_z = jnp.sum(weighted * delta_z - coef_three * weight_z, axis=(2, 3))
    return jnp.stack([field_x, field_y, field_z], axis=1)


def on_device(positions, polarizability, permanent_field, group_id, pair_mask):
    slabs = lax.axis_size(("blk", "oct", "sub"))
    member = lax.axis_index(("blk", "oct", "sub"))
    atom_count = positions.shape[1]
    length_z = layer_gap * atom_count * slabs / 256.0
    box_height = length_z / (BOXES_DEV * slabs)
    per_box = atom_count // BOXES_DEV
    width = (pair_mask.shape[1] - 1) // 2 * BLOCK
    group_limit = max(1, 32 // BOXES_DEV)
    static = jnp.concatenate(
        [positions, polarizability[None, :], group_id.astype(jnp.float32)[None, :]], axis=0
    )
    static_ext = padded(static, ((("blk", "oct", "sub"), 1),), width)
    own_boxes = member * BOXES_DEV + jnp.arange(BOXES_DEV, dtype=jnp.int32)
    interp = interpolation(positions.reshape(3, BOXES_DEV, per_box), own_boxes, box_height)
    surface = 4.0 * math.pi / 3.0 / (side_length * side_length * length_z)

    def induced(dipoles, total):
        dipole_ext = padded(dipoles, ((("blk", "oct", "sub"), 1),), width)
        near = near_total(static_ext, dipole_ext, pair_mask, length_z, atom_count)
        weights = jnp.einsum(
            "pba,cba->bcp", interp, dipoles.reshape(3, BOXES_DEV, per_box), precision=highest
        )
        piece = lax.all_gather(weights, ("blk", "oct", "sub"), axis=0, tiled=True)
        start = jnp.int32(0)
        count = piece.shape[0]
        size = split_size(count, group_limit)
        grouped = piece.reshape(count // size, size, 3, piece.shape[2])

        def visit(acc, item):
            index, bundle = item
            sources = start + index * size + jnp.arange(size, dtype=jnp.int32)
            return (acc + far_block(own_boxes, sources, bundle, slabs, box_height, length_z), None)

        result, unused = lax.scan(
            visit, jnp.zeros_like(weights), (jnp.arange(count // size, dtype=jnp.int32), grouped)
        )
        far = jnp.einsum("pba,bcp->cba", interp, result, precision=highest).reshape(3, atom_count)
        return near + far - surface * total[:, None]

    def moment(values):
        return lax.psum(jnp.sum(values, axis=1), ("blk", "oct", "sub"))

    def squares(resid, scaled):
        return lax.psum(jnp.sum(resid * scaled), ("blk", "oct", "sub"))

    dipoles = polarizability[None, :] * permanent_field
    residual = induced(dipoles, moment(dipoles))
    precond = polarizability[None, :] * residual
    direction = precond
    norm_now = squares(residual, precond)
    for step in range(ITERS):
        image = direction / polarizability[None, :] - induced(direction, moment(direction))
        rate = norm_now / lax.psum(jnp.sum(direction * image), ("blk", "oct", "sub"))
        dipoles = dipoles + rate * direction
        residual = residual - rate * image
        if step + 1 < ITERS:
            precond = polarizability[None, :] * residual
            norm_next = squares(residual, precond)
            direction = precond + norm_next / norm_now * direction
            norm_now = norm_next
    return (dipoles, residual)


def solution(mesh):
    return jax.shard_map(
        on_device,
        mesh=mesh,
        in_specs=(
            P(None, ("groups", "blk", "oct", "sub")),
            P(("groups", "blk", "oct", "sub")),
            P(None, ("groups", "blk", "oct", "sub")),
            P(("groups", "blk", "oct", "sub")),
            P(("groups", "blk", "oct", "sub"), None),
        ),
        out_specs=(
            P(None, ("groups", "blk", "oct", "sub")),
            P(None, ("groups", "blk", "oct", "sub")),
        ),
        check_vma=False,
    )
```

profile of v0, /device:TPU:0, one launch (start us, length us, event | category | flops | bytes accessed | tf_op | source)
XLA Modules:
  0.0 428.3 jit_solution(15247812564218952183)
XLA Ops:
  2.6 5.0 %collective-permute-start.2 = (f32[5,512]{1,0:T(8,128)S(1)}, f32[5,512]{1,0:T(8,128)S(1)}, u32[]{:S(2)}, u32[]{:S(2)}) collective-permute-start(f32[5,512]{1,0:T(8,128)S(1)} %get-tuple-element.990), channel_id=1, source_target_pairs={{1,0},{2,1},{3,2},{4,3},{5,4},{6,5},{7,6},{8,7},{9,8},{10,9},{11,1... | collective-permute-start | bytes 30728 | tf_op jit(solution)/shard_map/ppermute | solution.py:28
  8.6 4.4 %collective-permute-start.3 = (f32[3,512]{1,0:T(4,128)S(1)}, f32[3,512]{1,0:T(4,128)S(1)}, u32[]{:S(2)}, u32[]{:S(2)}) collective-permute-start(f32[3,512]{1,0:T(4,128)S(1)} %get-tuple-element.1086), channel_id=1, source_target_pairs={{1,0},{2,1},{3,2},{4,3},{5,4},{6,5},{7,6},{8,7},{9,8},{10,9},{11,1... | collective-permute-start | bytes 18440 | tf_op jit(solution)/shard_map/ppermute | solution.py:28
  14.0 29.5 %psum.49 = f32[3]{0:T(128)S(1)} all-reduce(f32[3]{0:T(128)S(1)} %get-tuple-element.927), channel_id=1, replica_groups=mesh['groups'=2,'blk'=4,'oct'=2,'sub'=2] {'blk','oct','sub'}, use_global_device_ids=true, to_apply=%region_33.34 | all-reduce | flops 3 | bytes 24 | tf_op jit(solution)/shard_map/psum | solution.py:210
  52.0 17.8 %all_gather.9 = f32[32,3,128]{2,1,0:T(4,128)S(1)} all-gather(f32[2,3,128]{2,1,0:T(4,128)S(1)} %fusion.782), channel_id=1, replica_groups=mesh['groups'=2,'blk'=4,'oct'=2,'sub'=2] {'blk','oct','sub'}, dimensions={0}, use_global_device_ids=true | all-gather | bytes 52224 | tf_op jit(solution)/shard_map/all_gather | solution.py:192
  69.9 13.5 %while.51 = (s32[]{:T(128)}, f32[2,3,128]{2,0,1:T(2,128)S(1)}, s32[2]{0:T(128)S(1)}, f32[2,16,3,128]{3,1,2,0:T(8,128)S(1)}, s32[]{:T(128)}, /*index=5*/s32[]{:T(...) while((s32[]{:T(128)}, f32[2,3,128]{2,0,1:T(2,128)S(1)}, ...), condition=%wide.region_31.32_spmd.clone.clone.clone.clone, body=%wide.region_27.31_spmd.sunk.clone.clone.clone.clone.sunk | while | flops 16765948 | bytes 2795035 | solution.py:203
  71.8 4.8 %subtract_reduce_fusion.9 = (f32[2,128]{1,0:T(2,128)S(1)}, f32[2,128]{1,0:T(2,128)S(1)}, f32[2,128]{1,0:T(2,128)S(1)}) fusion(f32[16,128]{1,0:T(8,128)S(1)} %get-tuple-element.1216, f32[128,128]{1,0:T(8,128)S(1)} %get-tuple-element.1217, pred[2,16]{1,0:T(4,128)(4,1)S(1)} %fusion.814, f32[16,128]{1,0:T(8,128)S(1)} %broadcast_add_fusion.12, ...), kind=kLoop, calls=%fused_computation.28.clone.1 | loop fusion | flops 15727872 | bytes 1282080 | tf_op jit(solution)/shard_map/while/body/eval_jaxpr/reduce_sum | solution.py:163
  78.5 4.8 %subtract_reduce_fusion.9 = (f32[2,128]{1,0:T(2,128)S(1)}, f32[2,128]{1,0:T(2,128)S(1)}, f32[2,128]{1,0:T(2,128)S(1)}) fusion(f32[16,128]{1,0:T(8,128)S(1)} %get-tuple-element.1216, f32[128,128]{1,0:T(8,128)S(1)} %get-tuple-element.1217, pred[2,16]{1,0:T(4,128)(4,1)S(1)} %fusion.814, f32[16,128]{1,0:T(8,128)S(1)} %broadcast_add_fusion.12, ...), kind=kLoop, calls=%fused_computation.28.clone.1 | loop fusion | flops 15727872 | bytes 1282080 | tf_op jit(solution)/shard_map/while/body/eval_jaxpr/reduce_sum | solution.py:163
  84.2 4.0 fusion.558
  88.2 4.0 fusion.585
  92.2 4.0 fusion.567
  96.2 4.0 fusion.576
  112.2 7.3 %fusion.630 = (f32[16,128]{1,0:T(8,128)S(1)}, f32[16,128]{1,0:T(8,128)S(1)}, f32[16,128]{1,0:T(8,128)S(1)}, f32[16,128]{1,0:T(8,128)S(1)}, f32[16,128]{1,0:T(8,128)S(1)}, /*index=5*/f32[16,128]{1,0:T(8,128)S(1)}) fusion(f32[16,128]{1,0:T(8,128)S(1)} %bitcast.840, f32[16,128]{1,0:T(8,128)S(1)} %bitcast.735, f32[16,128]{1,0:T(8,128)S(1)} %bitcast.931, ...), kind=kLoop, calls=%fused_computation.815 | loop fusion | flops 30920704 | bytes 180256 | tf_op jit(solution)/shard_map/reduce_sum | solution.py:70
  120.7 31.6 %psum.51 = f32[3]{0:T(128)S(1)} all-reduce(f32[3]{0:T(128)S(1)} %get-tuple-element.923), channel_id=1, replica_groups=mesh['groups'=2,'blk'=4,'oct'=2,'sub'=2] {'blk','oct','sub'}, use_global_device_ids=true, to_apply=%region_69.70 | all-reduce | flops 3 | bytes 24 | tf_op jit(solution)/shard_map/psum | solution.py:210
  153.2 4.4 %collective-permute-start.5 = (f32[3,512]{1,0:T(4,128)S(1)}, f32[3,512]{1,0:T(4,128)S(1)}, u32[]{:S(2)}, u32[]{:S(2)}) collective-permute-start(f32[3,512]{1,0:T(4,128)S(1)} %get-tuple-element.1078), channel_id=1, source_target_pairs={{1,0},{2,1},{3,2},{4,3},{5,4},{6,5},{7,6},{8,7},{9,8},{10,9},{11,1... | collective-permute-start | bytes 18440 | tf_op jit(solution)/shard_map/ppermute | solution.py:28
  157.6 17.3 %all_gather.10 = f32[32,3,128]{2,1,0:T(4,128)S(1)} all-gather(f32[2,3,128]{2,1,0:T(4,128)S(1)} %fusion.684), channel_id=1, replica_groups=mesh['groups'=2,'blk'=4,'oct'=2,'sub'=2] {'blk','oct','sub'}, dimensions={0}, use_global_device_ids=true | all-gather | bytes 52224 | tf_op jit(solution)/shard_map/all_gather | solution.py:192
  174.9 13.0 %while.52 = (s32[]{:T(128)}, f32[2,3,128]{2,0,1:T(2,128)S(1)}, s32[2]{0:T(128)S(1)}, f32[2,16,3,128]{3,1,2,0:T(8,128)S(1)}, s32[]{:T(128)}, /*index=5*/s32[]{:T(...) while((s32[]{:T(128)}, f32[2,3,128]{2,0,1:T(2,128)S(1)}, ...), condition=%wide.region_67.68_spmd.clone.clone.clone.clone, body=%wide.region_63.67_spmd.sunk.clone.clone.clone.clone.sunk | while | flops 16765948 | bytes 2795035 | solution.py:203
  176.6 4.8 %subtract_reduce_fusion.10 = (f32[2,128]{1,0:T(2,128)S(1)}, f32[2,128]{1,0:T(2,128)S(1)}, f32[2,128]{1,0:T(2,128)S(1)}) fusion(f32[16,128]{1,0:T(8,128)S(1)} %get-tuple-element.1230, f32[128,128]{1,0:T(8,128)S(1)} %get-tuple-element.1231, pred[2,16]{1,0:T(4,128)(4,1)S(1)} %fusion.817, f32[16,128]{1,0:T(8,128)S(1)} %broadcast_add_fusion.14, ...), kind=kLoop, calls=%fused_computation.82.clone.1 | loop fusion | flops 15727872 | bytes 1282080 | tf_op jit(solution)/shard_map/while/body/eval_jaxpr/reduce_sum | solution.py:163
  183.1 4.8 %subtract_reduce_fusion.10 = (f32[2,128]{1,0:T(2,128)S(1)}, f32[2,128]{1,0:T(2,128)S(1)}, f32[2,128]{1,0:T(2,128)S(1)}) fusion(f32[16,128]{1,0:T(8,128)S(1)} %get-tuple-element.1230, f32[128,128]{1,0:T(8,128)S(1)} %get-tuple-element.1231, pred[2,16]{1,0:T(4,128)(4,1)S(1)} %fusion.817, f32[16,128]{1,0:T(8,128)S(1)} %broadcast_add_fusion.14, ...), kind=kLoop, calls=%fused_computation.82.clone.1 | loop fusion | flops 15727872 | bytes 1282080 | tf_op jit(solution)/shard_map/while/body/eval_jaxpr/reduce_sum | solution.py:163
  200.1 4.0 fusion.557
  216.1 7.3 %fusion.629 = (f32[16,128]{1,0:T(8,128)S(1)}, f32[16,128]{1,0:T(8,128)S(1)}, f32[16,128]{1,0:T(8,128)S(1)}, f32[16,128]{1,0:T(8,128)S(1)}, f32[16,128]{1,0:T(8,128)S(1)}, /*index=5*/f32[16,128]{1,0:T(8,128)S(1)}) fusion(f32[16,128]{1,0:T(8,128)S(1)} %bitcast.872, f32[16,128]{1,0:T(8,128)S(1)} %bitcast.736, f32[16,128]{1,0:T(8,128)S(1)} %bitcast.939, ...), kind=kLoop, calls=%fused_computation.814 | loop fusion | flops 30920704 | bytes 180256 | tf_op jit(solution)/shard_map/reduce_sum | solution.py:70
  225.1 32.1 %all-reduce = (f32[]{:T(128)}, f32[]{:T(128)}) all-reduce(f32[]{:T(128)} %get-tuple-element.870, f32[]{:T(128)} %get-tuple-element.869), channel_id=1, replica_groups=mesh['groups'=2,'blk'=4,'oct'=2,'sub'=2] {'blk','oct','sub'}, use_global_device_ids=true, to_apply=%region_35.36 | all-reduce | flops 2 | bytes 16 | tf_op jit(solution)/shard_map/psum | solution.py:213
  259.1 30.1 %psum.53 = f32[]{:T(128)} all-reduce(f32[]{:T(128)} %fusion.632), channel_id=1, replica_groups=mesh['groups'=2,'blk'=4,'oct'=2,'sub'=2] {'blk','oct','sub'}, use_global_device_ids=true, to_apply=%region_73.74 | all-reduce | flops 1 | bytes 8 | tf_op jit(solution)/shard_map/psum | solution.py:213
  290.6 29.7 %psum.54 = f32[3]{0:T(128)S(1)} all-reduce(f32[3]{0:T(128)S(1)} %get-tuple-element.918), channel_id=1, replica_groups=mesh['groups'=2,'blk'=4,'oct'=2,'sub'=2] {'blk','oct','sub'}, use_global_device_ids=true, to_apply=%region_107.108 | all-reduce | flops 3 | bytes 24 | tf_op jit(solution)/shard_map/psum | solution.py:210
  321.3 4.4 %collective-permute-start.7 = (f32[3,512]{1,0:T(4,128)S(1)}, f32[3,512]{1,0:T(4,128)S(1)}, u32[]{:S(2)}, u32[]{:S(2)}) collective-permute-start(f32[3,512]{1,0:T(4,128)S(1)} %get-tuple-element.1070), channel_id=1, source_target_pairs={{1,0},{2,1},{3,2},{4,3},{5,4},{6,5},{7,6},{8,7},{9,8},{10,9},{11,1... | collective-permute-start | bytes 18440 | tf_op jit(solution)/shard_map/ppermute | solution.py:28
  325.7 17.3 %all_gather.11 = f32[32,3,128]{2,1,0:T(4,128)S(1)} all-gather(f32[2,3,128]{2,1,0:T(4,128)S(1)} %fusion.783), channel_id=1, replica_groups=mesh['groups'=2,'blk'=4,'oct'=2,'sub'=2] {'blk','oct','sub'}, dimensions={0}, use_global_device_ids=true | all-gather | bytes 52224 | tf_op jit(solution)/shard_map/all_gather | solution.py:192
  343.0 13.0 %while.53 = (s32[]{:T(128)}, f32[2,3,128]{2,0,1:T(2,128)S(1)}, s32[2]{0:T(128)S(1)}, f32[2,16,3,128]{3,1,2,0:T(8,128)S(1)}, s32[]{:T(128)}, /*index=5*/s32[]{:T(...) while((s32[]{:T(128)}, f32[2,3,128]{2,0,1:T(2,128)S(1)}, ...), condition=%wide.region_105.106_spmd.clone.clone.clone.clone, body=%wide.region_101.105_spmd.sunk.clone.clone.clone.clone.sunk | while | flops 16765948 | bytes 2795035 | solution.py:203
  344.7 4.8 %subtract_reduce_fusion.11 = (f32[2,128]{1,0:T(2,128)S(1)}, f32[2,128]{1,0:T(2,128)S(1)}, f32[2,128]{1,0:T(2,128)S(1)}) fusion(f32[16,128]{1,0:T(8,128)S(1)} %get-tuple-element.1244, f32[128,128]{1,0:T(8,128)S(1)} %get-tuple-element.1245, pred[2,16]{1,0:T(4,128)(4,1)S(1)} %fusion.820, f32[16,128]{1,0:T(8,128)S(1)} %broadcast_add_fusion.16, ...), kind=kLoop, calls=%fused_computation.136.clone.1 | loop fusion | flops 15727872 | bytes 1282080 | tf_op jit(solution)/shard_map/while/body/eval_jaxpr/reduce_sum | solution.py:163
  351.2 4.8 %subtract_reduce_fusion.11 = (f32[2,128]{1,0:T(2,128)S(1)}, f32[2,128]{1,0:T(2,128)S(1)}, f32[2,128]{1,0:T(2,128)S(1)}) fusion(f32[16,128]{1,0:T(8,128)S(1)} %get-tuple-element.1244, f32[128,128]{1,0:T(8,128)S(1)} %get-tuple-element.1245, pred[2,16]{1,0:T(4,128)(4,1)S(1)} %fusion.820, f32[16,128]{1,0:T(8,128)S(1)} %broadcast_add_fusion.16, ...), kind=kLoop, calls=%fused_computation.136.clone.1 | loop fusion | flops 15727872 | bytes 1282080 | tf_op jit(solution)/shard_map/while/body/eval_jaxpr/reduce_sum | solution.py:163
  368.2 4.0 fusion.574
  376.2 4.0 fusion.610
  384.3 7.3 %fusion.628 = (f32[16,128]{1,0:T(8,128)S(1)}, f32[16,128]{1,0:T(8,128)S(1)}, f32[16,128]{1,0:T(8,128)S(1)}, f32[16,128]{1,0:T(8,128)S(1)}, f32[16,128]{1,0:T(8,128)S(1)}, /*index=5*/f32[16,128]{1,0:T(8,128)S(1)}) fusion(f32[16,128]{1,0:T(8,128)S(1)} %bitcast.862, f32[16,128]{1,0:T(8,128)S(1)} %bitcast.737, f32[16,128]{1,0:T(8,128)S(1)} %bitcast.947, ...), kind=kLoop, calls=%fused_computation.813 | loop fusion | flops 30920704 | bytes 180256 | tf_op jit(solution)/shard_map/reduce_sum | solution.py:70
  393.2 32.0 %psum.55 = f32[]{:T(128)} all-reduce(f32[]{:T(128)} %get-tuple-element.1104), channel_id=1, replica_groups=mesh['groups'=2,'blk'=4,'oct'=2,'sub'=2] {'blk','oct','sub'}, use_global_device_ids=true, to_apply=%region_109.110 | all-reduce | flops 1 | bytes 8 | tf_op jit(solution)/shard_map/psum | solution.py:222
  (190 shorter events, 84.4 us)
Async XLA Ops:
  0.6 45.0 %copy-start.8 = (f32[5,5,1]{1,0,2:T(8,128)S(1)}, f32[5,5,1]{1,0,2:T(8,128)}, u32[]{:S(2)}) copy-start(f32[5,5,1]{1,0,2:T(8,128)} %constant.532) | copy-start | bytes 304
  0.6 45.2 %copy-start.11 = (f32[128,5,1]{0,1,2:T(8,128)S(1)}, f32[128,5,1]{0,1,2:T(8,128)}, u32[]{:S(2)}) copy-start(f32[128,5,1]{0,1,2:T(8,128)} %constant.533) | copy-start | bytes 7684
  2.1 81.8 %collective-permute-start = (f32[5,512]{1,0:T(8,128)S(1)}, f32[5,512]{1,0:T(8,128)S(1)}, u32[]{:S(2)}, u32[]{:S(2)}) collective-permute-start(f32[5,512]{1,0:T(8,128)S(1)} %get-tuple-element.989), channel_id=1, source_target_pairs={{0,1},{1,2},{2,3},{3,4},{4,5},{5,6},{6,7},{7,8},{8,9},{9,10},{10,1... | collective-permute-start | bytes 30728 | tf_op jit(solution)/shard_map/ppermute | solution.py:26
  2.6 81.3 %collective-permute-start.2 = (f32[5,512]{1,0:T(8,128)S(1)}, f32[5,512]{1,0:T(8,128)S(1)}, u32[]{:S(2)}, u32[]{:S(2)}) collective-permute-start(f32[5,512]{1,0:T(8,128)S(1)} %get-tuple-element.990), channel_id=1, source_target_pairs={{1,0},{2,1},{3,2},{4,3},{5,4},{6,5},{7,6},{8,7},{9,8},{10,9},{11,1... | collective-permute-start | bytes 30728 | tf_op jit(solution)/shard_map/ppermute | solution.py:28
  8.6 75.2 %collective-permute-start.1 = (f32[3,512]{1,0:T(4,128)S(1)}, f32[3,512]{1,0:T(4,128)S(1)}, u32[]{:S(2)}, u32[]{:S(2)}) collective-permute-start(f32[3,512]{1,0:T(4,128)S(1)} %get-tuple-element.1085), channel_id=1, source_target_pairs={{0,1},{1,2},{2,3},{3,4},{4,5},{5,6},{6,7},{7,8},{8,9},{9,10},{10,1... | collective-permute-start | bytes 18440 | tf_op jit(solution)/shard_map/ppermute | solution.py:26
  8.6 75.2 %collective-permute-start.3 = (f32[3,512]{1,0:T(4,128)S(1)}, f32[3,512]{1,0:T(4,128)S(1)}, u32[]{:S(2)}, u32[]{:S(2)}) collective-permute-start(f32[3,512]{1,0:T(4,128)S(1)} %get-tuple-element.1086), channel_id=1, source_target_pairs={{1,0},{2,1},{3,2},{4,3},{5,4},{6,5},{7,6},{8,7},{9,8},{10,9},{11,1... | collective-permute-start | bytes 18440 | tf_op jit(solution)/shard_map/ppermute | solution.py:28
  13.1 34.7 %copy-start.10 = (f32[128,5,1]{0,1,2:T(8,128)S(1)}, f32[128,5,1]{0,1,2:T(8,128)}, u32[]{:S(2)}) copy-start(f32[128,5,1]{0,1,2:T(8,128)} %constant.534) | copy-start | bytes 7684
  47.7 1.8 copy-start.9
  51.4 18.4 %copy-start.2 = (f32[128]{0:T(128)S(1)}, f32[128]{0:T(128)}, u32[]{:S(2)}) copy-start(f32[128]{0:T(128)} %constant.2011) | copy-start | bytes 1540
  51.4 18.4 %copy-start.4 = (f32[128]{0:T(128)S(1)}, f32[128]{0:T(128)}, u32[]{:S(2)}) copy-start(f32[128]{0:T(128)} %constant.489.clone..sunk.15) | copy-start | bytes 1540
  51.4 18.4 %copy-start.5 = (f32[128]{0:T(128)S(1)}, f32[128]{0:T(128)}, u32[]{:S(2)}) copy-start(f32[128]{0:T(128)} %constant.2010) | copy-start | bytes 1540
  51.4 18.4 %copy-start.6 = (f32[128]{0:T(128)S(1)}, f32[128]{0:T(128)}, u32[]{:S(2)}) copy-start(f32[128]{0:T(128)} %constant.490.clone..sunk.15) | copy-start | bytes 1540
  51.4 18.4 %copy-start.7 = (f32[128]{0:T(128)S(1)}, f32[128]{0:T(128)}, u32[]{:S(2)}) copy-start(f32[128]{0:T(128)} %constant.2009) | copy-start | bytes 1540
  69.9 13.5 %copy-start = (s32[16,9]{1,0:T(8,128)S(1)}, s32[16,9]{1,0:T(8,128)}, u32[]{:S(2)}) copy-start(s32[16,9]{1,0:T(8,128)} %param.28) | copy-start | bytes 1732
  69.9 13.8 %copy-start.1 = (f32[2048]{0:T(1024)S(1)}, f32[2048]{0:T(1024)}, u32[]{:S(2)}) copy-start(f32[2048]{0:T(1024)} %param.25) | copy-start | bytes 24580
  69.9 14.0 %copy-start.3 = (f32[3,2048]{1,0:T(4,128)S(1)}, f32[3,2048]{1,0:T(4,128)}, u32[]{:S(2)}) copy-start(f32[3,2048]{1,0:T(4,128)} %param.24) | copy-start | bytes 73732
  153.1 34.8 %collective-permute-start.4 = (f32[3,512]{1,0:T(4,128)S(1)}, f32[3,512]{1,0:T(4,128)S(1)}, u32[]{:S(2)}, u32[]{:S(2)}) collective-permute-start(f32[3,512]{1,0:T(4,128)S(1)} %get-tuple-element.1077), channel_id=1, source_target_pairs={{0,1},{1,2},{2,3},{3,4},{4,5},{5,6},{6,7},{7,8},{8,9},{9,10},{10,1... | collective-permute-start | bytes 18440 | tf_op jit(solution)/shard_map/ppermute | solution.py:26
  153.2 34.8 %collective-permute-start.5 = (f32[3,512]{1,0:T(4,128)S(1)}, f32[3,512]{1,0:T(4,128)S(1)}, u32[]{:S(2)}, u32[]{:S(2)}) collective-permute-start(f32[3,512]{1,0:T(4,128)S(1)} %get-tuple-element.1078), channel_id=1, source_target_pairs={{1,0},{2,1},{3,2},{4,3},{5,4},{6,5},{7,6},{8,7},{9,8},{10,9},{11,1... | collective-permute-start | bytes 18440 | tf_op jit(solution)/shard_map/ppermute | solution.py:28
  321.2 34.8 %collective-permute-start.6 = (f32[3,512]{1,0:T(4,128)S(1)}, f32[3,512]{1,0:T(4,128)S(1)}, u32[]{:S(2)}, u32[]{:S(2)}) collective-permute-start(f32[3,512]{1,0:T(4,128)S(1)} %get-tuple-element.1069), channel_id=1, source_target_pairs={{0,1},{1,2},{2,3},{3,4},{4,5},{5,6},{6,7},{7,8},{8,9},{9,10},{10,1... | collective-permute-start | bytes 18440 | tf_op jit(solution)/shard_map/ppermute | solution.py:26
  321.3 34.8 %collective-permute-start.7 = (f32[3,512]{1,0:T(4,128)S(1)}, f32[3,512]{1,0:T(4,128)S(1)}, u32[]{:S(2)}, u32[]{:S(2)}) collective-permute-start(f32[3,512]{1,0:T(4,128)S(1)} %get-tuple-element.1070), channel_id=1, source_target_pairs={{1,0},{2,1},{3,2},{4,3},{5,4},{6,5},{7,6},{8,7},{9,8},{10,9},{11,1... | collective-permute-start | bytes 18440 | tf_op jit(solution)/shard_map/ppermute | solution.py:28
where the time goes:
time: 434 us; the launch traced here: 428 us
  blocking collectives  237 us (55%)
  other arithmetic  145 us (33%)
  starting transfers between devices  19 us (4%)
  matrix products  13.6 us (3%)
  between operations  5.61 us (1%)
    reduce_sum x24, other arithmetic, near_tiles(): jnp.sum(weighted * delta_x - coef_three * moments[0][:, None, :], axis=2)  106 us
    psum x3, blocking collectives, moment(): return lax.psum(jnp.sum(values, axis=1), ('blk', 'oct', 'sub'))  90.8 us
    psum x2, blocking collectives, squares(): return lax.psum(jnp.sum(resid * scaled), ('blk', 'oct', 'sub'))  62.2 us
    all_gather x3, blocking collectives, induced(): piece = lax.all_gather(weights, ('blk', 'oct', 'sub'), axis=0, tiled=True)  52.3 us
    psum x1, blocking collectives, on_device(): lax.psum(jnp.sum(direction * image), ('blk', 'oct', 'sub'))  32 us
    reduce_sum x6, other arithmetic, far_block(): field_x = jnp.sum(weighted * delta_x - coef_three * weight_x, axis=(2, 3))  28.8 us
    ppermute x4, starting transfers between devices, padded(): lax.ppermute(head, axis, [((i + 1) % count, i) for i in range(count)])  18.3 us
  transfers between devices with their start and end apart: 8, of which 0 were waited for; matrix products, arithmetic and copies ran while one was open for 11% of the time, Pallas kernels for 0%

commit v1 on v0

--- a/solution.py
+++ b/solution.py
@@ -1,3 +1,4 @@
+import functools
 import math
 import jax
 import jax.numpy as jnp
@@ -14,6 +15,14 @@
 layer_gap = 2.5
 thole_damp = 0.39
 highest = lax.Precision.HIGHEST
+
+
+def extend_side_on_mesh(here_x, axis_id, along_axis):
+    new = jax.lax.psum(here_x, axis_name=axis_id)
+    return jax.lax.psum(new, along_axis)
+
+
+scan_row = functools.partial(extend_side_on_mesh, axis_id=("oct", "sub"), along_axis="blk")
 
 
 def padded(cells, sides, width):
@@ -207,7 +216,7 @@
         return near + far - surface * total[:, None]
 
     def moment(values):
-        return lax.psum(jnp.sum(values, axis=1), ("blk", "oct", "sub"))
+        return scan_row(jnp.sum(values, axis=1))
 
     def squares(resid, scaled):
         return lax.psum(jnp.sum(resid * scaled), ("blk", "oct", "sub"))

time: 434 us -> 390 us (0.90)
  blocking collectives: 237 us -> 192 us
    psum x3 -> x6, blocking collectives: 90.8 us -> 44.9 us  [the longest x3 26.5 us: extend_side_on_mesh(): return jax.lax.psum(new, along_axis)]
  transfers between devices with their start and end apart: 8 -> 8, of which waited for: 0 -> 0; matrix products, arithmetic and copies ran while one was open for 11% -> 12% of each run, Pallas kernels for 0% -> 0%
where the time goes in v1:
time: 390 us; the launch traced here: 384 us
  blocking collectives  192 us (49%)
  other arithmetic  145 us (37%)
  starting transfers between devices  19 us (5%)
  matrix products  13.6 us (3%)
  between operations  5.71 us (1%)
  local copies, waits for them, and re-layouts  4.59 us (1%)
  loops' own time  4.47 us (1%)
    reduce_sum x24, other arithmetic, near_tiles(): jnp.sum(weighted * delta_x - coef_three * moments[0][:, None, :], axis=2)  106 us
    psum x2, blocking collectives, squares(): return lax.psum(jnp.sum(resid * scaled), ('blk', 'oct', 'sub'))  62.2 us
    all_gather x3, blocking collectives, induced(): piece = lax.all_gather(weights, ('blk', 'oct', 'sub'), axis=0, tiled=True)  53.4 us
    psum x1, blocking collectives, on_device(): lax.psum(jnp.sum(direction * image), ('blk', 'oct', 'sub'))  31.7 us
    reduce_sum x6, other arithmetic, far_block(): field_x = jnp.sum(weighted * delta_x - coef_three * weight_x, axis=(2, 3))  28.8 us
    psum x3, blocking collectives, extend_side_on_mesh(): return jax.lax.psum(new, along_axis)  26.5 us
    psum x3, blocking collectives, extend_side_on_mesh(): new = jax.lax.psum(here_x, axis_name=axis_id)  18.4 us
    ppermute x4, starting transfers between devices, padded(): lax.ppermute(head, axis, [((i + 1) % count, i) for i in range(count)])  18.3 us
  transfers between devices with their start and end apart: 8, of which 0 were waited for; matrix products, arithmetic and copies ran while one was open for 12% of the time, Pallas kernels for 0%

profile of v1, /device:TPU:0, one launch (start us, length us, event | category | flops | bytes accessed | tf_op | source)
XLA Modules:
  0.0 384.1 jit_solution(16571897744576913671)
XLA Ops:
  2.6 5.0 %collective-permute-start.2 = (f32[5,512]{1,0:T(8,128)S(1)}, f32[5,512]{1,0:T(8,128)S(1)}, u32[]{:S(2)}, u32[]{:S(2)}) collective-permute-start(f32[5,512]{1,0:T(8,128)S(1)} %get-tuple-element.990), channel_id=1, source_target_pairs={{1,0},{2,1},{3,2},{4,3},{5,4},{6,5},{7,6},{8,7},{9,8},{10,9},{11,1... | collective-permute-start | bytes 30728 | tf_op jit(solution)/shard_map/ppermute | solution.py:37
  8.6 4.4 %collective-permute-start.3 = (f32[3,512]{1,0:T(4,128)S(1)}, f32[3,512]{1,0:T(4,128)S(1)}, u32[]{:S(2)}, u32[]{:S(2)}) collective-permute-start(f32[3,512]{1,0:T(4,128)S(1)} %get-tuple-element.1086), channel_id=1, source_target_pairs={{1,0},{2,1},{3,2},{4,3},{5,4},{6,5},{7,6},{8,7},{9,8},{10,9},{11,1... | collective-permute-start | bytes 18440 | tf_op jit(solution)/shard_map/ppermute | solution.py:37
  14.0 5.8 %psum.70 = f32[3]{0:T(128)S(1)} all-reduce(f32[3]{0:T(128)S(1)} %get-tuple-element.927), channel_id=1, replica_groups=mesh['groups'=2,'blk'=4,'oct'=2,'sub'=2] {'oct','sub'}, use_global_device_ids=true, to_apply=%region_33.34 | all-reduce | flops 3 | bytes 24 | tf_op jit(solution)/shard_map/psum | solution.py:21
  19.7 8.8 %psum.71 = f32[3]{0:T(128)S(1)} all-reduce(f32[3]{0:T(128)S(1)} %psum.70), channel_id=1, replica_groups=mesh['groups'=2,'blk'=4,'oct'=2,'sub'=2] {'blk'}, use_global_device_ids=true, to_apply=%region_34.35 | all-reduce | flops 3 | bytes 24 | tf_op jit(solution)/shard_map/psum | solution.py:22
  37.1 18.5 %all_gather.9 = f32[32,3,128]{2,1,0:T(4,128)S(1)} all-gather(f32[2,3,128]{2,1,0:T(4,128)S(1)} %fusion.782), channel_id=1, replica_groups=mesh['groups'=2,'blk'=4,'oct'=2,'sub'=2] {'blk','oct','sub'}, dimensions={0}, use_global_device_ids=true | all-gather | bytes 52224 | tf_op jit(solution)/shard_map/all_gather | solution.py:201
  55.7 13.5 %while.51 = (s32[]{:T(128)}, f32[2,3,128]{2,0,1:T(2,128)S(1)}, s32[2]{0:T(128)S(1)}, f32[2,16,3,128]{3,1,2,0:T(8,128)S(1)}, s32[]{:T(128)}, /*index=5*/s32[]{:T(...) while((s32[]{:T(128)}, f32[2,3,128]{2,0,1:T(2,128)S(1)}, ...), condition=%wide.region_31.32_spmd.clone.clone.clone.clone, body=%wide.region_27.31_spmd.sunk.clone.clone.clone.clone.sunk | while | flops 16765948 | bytes 2795035 | solution.py:212
  57.6 4.8 %subtract_reduce_fusion.9 = (f32[2,128]{1,0:T(2,128)S(1)}, f32[2,128]{1,0:T(2,128)S(1)}, f32[2,128]{1,0:T(2,128)S(1)}) fusion(f32[16,128]{1,0:T(8,128)S(1)} %get-tuple-element.1216, f32[128,128]{1,0:T(8,128)S(1)} %get-tuple-element.1217, pred[2,16]{1,0:T(4,128)(4,1)S(1)} %fusion.814, f32[16,128]{1,0:T(8,128)S(1)} %broadcast_add_fusion.12, ...), kind=kLoop, calls=%fused_computation.28.clone.1 | loop fusion | flops 15727872 | bytes 1282080 | tf_op jit(solution)/shard_map/while/body/eval_jaxpr/reduce_sum | solution.py:172
  64.4 4.8 %subtract_reduce_fusion.9 = (f32[2,128]{1,0:T(2,128)S(1)}, f32[2,128]{1,0:T(2,128)S(1)}, f32[2,128]{1,0:T(2,128)S(1)}) fusion(f32[16,128]{1,0:T(8,128)S(1)} %get-tuple-element.1216, f32[128,128]{1,0:T(8,128)S(1)} %get-tuple-element.1217, pred[2,16]{1,0:T(4,128)(4,1)S(1)} %fusion.814, f32[16,128]{1,0:T(8,128)S(1)} %broadcast_add_fusion.12, ...), kind=kLoop, calls=%fused_computation.28.clone.1 | loop fusion | flops 15727872 | bytes 1282080 | tf_op jit(solution)/shard_map/while/body/eval_jaxpr/reduce_sum | solution.py:172
  74.0 4.0 %fusion.585 = (f32[16,128]{1,0:T(8,128)S(1)}, f32[16,128]{1,0:T(8,128)S(1)}, f32[16,128]{1,0:T(8,128)S(1)}) fusion(f32[16,128]{1,0:T(8,128)S(1)} %bitcast.857, f32[16,128]{1,0:T(8,128)S(1)} %bitcast.897, f32[16,128]{1,0:T(8,128)S(1)} %bitcast.925, f32[16,128]{1,0:T(8,128)S(1)} %bitcast.706, f32[16,128]{1,0:T(8,128)S(1)} %bitcast.705, ...), kind=kLoop, calls=%fused_computation.770 | loop fusion | flops 15460352 | bytes 131088 | tf_op jit(solution)/shard_map/reduce_sum | solution.py:79
  82.0 4.0 %fusion.576 = (f32[16,128]{1,0:T(8,128)S(1)}, f32[16,128]{1,0:T(8,128)S(1)}, f32[16,128]{1,0:T(8,128)S(1)}) fusion(f32[16,128]{1,0:T(8,128)S(1)} %bitcast.699, f32[16,128]{1,0:T(8,128)S(1)} %bitcast.789, f32[16,128]{1,0:T(8,128)S(1)} %bitcast.927, f32[16,128]{1,0:T(8,128)S(1)} %bitcast.701, f32[16,128]{1,0:T(8,128)S(1)} %bitcast.700, ...), kind=kLoop, calls=%fused_computation.761 | loop fusion | flops 15460352 | bytes 131088 | tf_op jit(solution)/shard_map/reduce_sum | solution.py:79
  98.1 7.3 %fusion.630 = (f32[16,128]{1,0:T(8,128)S(1)}, f32[16,128]{1,0:T(8,128)S(1)}, f32[16,128]{1,0:T(8,128)S(1)}, f32[16,128]{1,0:T(8,128)S(1)}, f32[16,128]{1,0:T(8,128)S(1)}, /*index=5*/f32[16,128]{1,0:T(8,128)S(1)}) fusion(f32[16,128]{1,0:T(8,128)S(1)} %bitcast.840, f32[16,128]{1,0:T(8,128)S(1)} %bitcast.735, f32[16,128]{1,0:T(8,128)S(1)} %bitcast.931, ...), kind=kLoop, calls=%fused_computation.815 | loop fusion | flops 30920704 | bytes 180256 | tf_op jit(solution)/shard_map/reduce_sum | solution.py:79
  106.5 6.9 %psum.73 = f32[3]{0:T(128)S(1)} all-reduce(f32[3]{0:T(128)S(1)} %get-tuple-element.923), channel_id=1, replica_groups=mesh['groups'=2,'blk'=4,'oct'=2,'sub'=2] {'oct','sub'}, use_global_device_ids=true, to_apply=%region_70.71 | all-reduce | flops 3 | bytes 24 | tf_op jit(solution)/shard_map/psum | solution.py:21
  113.3 9.1 %psum.74 = f32[3]{0:T(128)S(1)} all-reduce(f32[3]{0:T(128)S(1)} %psum.73), channel_id=1, replica_groups=mesh['groups'=2,'blk'=4,'oct'=2,'sub'=2] {'blk'}, use_global_device_ids=true, to_apply=%region_71.72 | all-reduce | flops 3 | bytes 24 | tf_op jit(solution)/shard_map/psum | solution.py:22
  123.3 4.4 %collective-permute-start.5 = (f32[3,512]{1,0:T(4,128)S(1)}, f32[3,512]{1,0:T(4,128)S(1)}, u32[]{:S(2)}, u32[]{:S(2)}) collective-permute-start(f32[3,512]{1,0:T(4,128)S(1)} %get-tuple-element.1078), channel_id=1, source_target_pairs={{1,0},{2,1},{3,2},{4,3},{5,4},{6,5},{7,6},{8,7},{9,8},{10,9},{11,1... | collective-permute-start | bytes 18440 | tf_op jit(solution)/shard_map/ppermute | solution.py:37
  127.8 17.3 %all_gather.10 = f32[32,3,128]{2,1,0:T(4,128)S(1)} all-gather(f32[2,3,128]{2,1,0:T(4,128)S(1)} %fusion.684), channel_id=1, replica_groups=mesh['groups'=2,'blk'=4,'oct'=2,'sub'=2] {'blk','oct','sub'}, dimensions={0}, use_global_device_ids=true | all-gather | bytes 52224 | tf_op jit(solution)/shard_map/all_gather | solution.py:201
  145.1 13.5 %while.52 = (s32[]{:T(128)}, f32[2,3,128]{2,0,1:T(2,128)S(1)}, s32[2]{0:T(128)S(1)}, f32[2,16,3,128]{3,1,2,0:T(8,128)S(1)}, s32[]{:T(128)}, /*index=5*/s32[]{:T(...) while((s32[]{:T(128)}, f32[2,3,128]{2,0,1:T(2,128)S(1)}, ...), condition=%wide.region_68.69_spmd.clone.clone.clone.clone, body=%wide.region_64.68_spmd.sunk.clone.clone.clone.clone.sunk | while | flops 16765948 | bytes 2795035 | solution.py:212
  147.0 4.8 %subtract_reduce_fusion.10 = (f32[2,128]{1,0:T(2,128)S(1)}, f32[2,128]{1,0:T(2,128)S(1)}, f32[2,128]{1,0:T(2,128)S(1)}) fusion(f32[16,128]{1,0:T(8,128)S(1)} %get-tuple-element.1230, f32[128,128]{1,0:T(8,128)S(1)} %get-tuple-element.1231, pred[2,16]{1,0:T(4,128)(4,1)S(1)} %fusion.817, f32[16,128]{1,0:T(8,128)S(1)} %broadcast_add_fusion.14, ...), kind=kLoop, calls=%fused_computation.82.clone.1 | loop fusion | flops 15727872 | bytes 1282080 | tf_op jit(solution)/shard_map/while/body/eval_jaxpr/reduce_sum | solution.py:172
  153.7 4.8 %subtract_reduce_fusion.10 = (f32[2,128]{1,0:T(2,128)S(1)}, f32[2,128]{1,0:T(2,128)S(1)}, f32[2,128]{1,0:T(2,128)S(1)}) fusion(f32[16,128]{1,0:T(8,128)S(1)} %get-tuple-element.1230, f32[128,128]{1,0:T(8,128)S(1)} %get-tuple-element.1231, pred[2,16]{1,0:T(4,128)(4,1)S(1)} %fusion.817, f32[16,128]{1,0:T(8,128)S(1)} %broadcast_add_fusion.14, ...), kind=kLoop, calls=%fused_computation.82.clone.1 | loop fusion | flops 15727872 | bytes 1282080 | tf_op jit(solution)/shard_map/while/body/eval_jaxpr/reduce_sum | solution.py:172
  186.7 7.3 %fusion.629 = (f32[16,128]{1,0:T(8,128)S(1)}, f32[16,128]{1,0:T(8,128)S(1)}, f32[16,128]{1,0:T(8,128)S(1)}, f32[16,128]{1,0:T(8,128)S(1)}, f32[16,128]{1,0:T(8,128)S(1)}, /*index=5*/f32[16,128]{1,0:T(8,128)S(1)}) fusion(f32[16,128]{1,0:T(8,128)S(1)} %bitcast.872, f32[16,128]{1,0:T(8,128)S(1)} %bitcast.736, f32[16,128]{1,0:T(8,128)S(1)} %bitcast.939, ...), kind=kLoop, calls=%fused_computation.814 | loop fusion | flops 30920704 | bytes 180256 | tf_op jit(solution)/shard_map/reduce_sum | solution.py:79
  195.7 32.1 %all-reduce = (f32[]{:T(128)}, f32[]{:T(128)}) all-reduce(f32[]{:T(128)} %get-tuple-element.870, f32[]{:T(128)} %get-tuple-element.869), channel_id=1, replica_groups=mesh['groups'=2,'blk'=4,'oct'=2,'sub'=2] {'blk','oct','sub'}, use_global_device_ids=true, to_apply=%region_36.37 | all-reduce | flops 2 | bytes 16 | tf_op jit(solution)/shard_map/psum | solution.py:222
  229.8 30.1 %psum.76 = f32[]{:T(128)} all-reduce(f32[]{:T(128)} %fusion.632), channel_id=1, replica_groups=mesh['groups'=2,'blk'=4,'oct'=2,'sub'=2] {'blk','oct','sub'}, use_global_device_ids=true, to_apply=%region_75.76 | all-reduce | flops 1 | bytes 8 | tf_op jit(solution)/shard_map/psum | solution.py:222
  261.4 5.8 %psum.77 = f32[3]{0:T(128)S(1)} all-reduce(f32[3]{0:T(128)S(1)} %get-tuple-element.918), channel_id=1, replica_groups=mesh['groups'=2,'blk'=4,'oct'=2,'sub'=2] {'oct','sub'}, use_global_device_ids=true, to_apply=%region_109.110 | all-reduce | flops 3 | bytes 24 | tf_op jit(solution)/shard_map/psum | solution.py:21
  267.2 8.6 %psum.78 = f32[3]{0:T(128)S(1)} all-reduce(f32[3]{0:T(128)S(1)} %psum.77), channel_id=1, replica_groups=mesh['groups'=2,'blk'=4,'oct'=2,'sub'=2] {'blk'}, use_global_device_ids=true, to_apply=%region_110.111 | all-reduce | flops 3 | bytes 24 | tf_op jit(solution)/shard_map/psum | solution.py:22
  276.7 4.4 %collective-permute-start.7 = (f32[3,512]{1,0:T(4,128)S(1)}, f32[3,512]{1,0:T(4,128)S(1)}, u32[]{:S(2)}, u32[]{:S(2)}) collective-permute-start(f32[3,512]{1,0:T(4,128)S(1)} %get-tuple-element.1070), channel_id=1, source_target_pairs={{1,0},{2,1},{3,2},{4,3},{5,4},{6,5},{7,6},{8,7},{9,8},{10,9},{11,1... | collective-permute-start | bytes 18440 | tf_op jit(solution)/shard_map/ppermute | solution.py:37
  281.1 17.6 %all_gather.11 = f32[32,3,128]{2,1,0:T(4,128)S(1)} all-gather(f32[2,3,128]{2,1,0:T(4,128)S(1)} %fusion.783), channel_id=1, replica_groups=mesh['groups'=2,'blk'=4,'oct'=2,'sub'=2] {'blk','oct','sub'}, dimensions={0}, use_global_device_ids=true | all-gather | bytes 52224 | tf_op jit(solution)/shard_map/all_gather | solution.py:201
  298.7 13.5 %while.53 = (s32[]{:T(128)}, f32[2,3,128]{2,0,1:T(2,128)S(1)}, s32[2]{0:T(128)S(1)}, f32[2,16,3,128]{3,1,2,0:T(8,128)S(1)}, s32[]{:T(128)}, /*index=5*/s32[]{:T(...) while((s32[]{:T(128)}, f32[2,3,128]{2,0,1:T(2,128)S(1)}, ...), condition=%wide.region_107.108_spmd.clone.clone.clone.clone, body=%wide.region_103.107_spmd.sunk.clone.clone.clone.clone.sunk | while | flops 16765948 | bytes 2795035 | solution.py:212
  300.6 4.8 %subtract_reduce_fusion.11 = (f32[2,128]{1,0:T(2,128)S(1)}, f32[2,128]{1,0:T(2,128)S(1)}, f32[2,128]{1,0:T(2,128)S(1)}) fusion(f32[16,128]{1,0:T(8,128)S(1)} %get-tuple-element.1244, f32[128,128]{1,0:T(8,128)S(1)} %get-tuple-element.1245, pred[2,16]{1,0:T(4,128)(4,1)S(1)} %fusion.820, f32[16,128]{1,0:T(8,128)S(1)} %broadcast_add_fusion.16, ...), kind=kLoop, calls=%fused_computation.136.clone.1 | loop fusion | flops 15727872 | bytes 1282080 | tf_op jit(solution)/shard_map/while/body/eval_jaxpr/reduce_sum | solution.py:172
  307.4 4.8 %subtract_reduce_fusion.11 = (f32[2,128]{1,0:T(2,128)S(1)}, f32[2,128]{1,0:T(2,128)S(1)}, f32[2,128]{1,0:T(2,128)S(1)}) fusion(f32[16,128]{1,0:T(8,128)S(1)} %get-tuple-element.1244, f32[128,128]{1,0:T(8,128)S(1)} %get-tuple-element.1245, pred[2,16]{1,0:T(4,128)(4,1)S(1)} %fusion.820, f32[16,128]{1,0:T(8,128)S(1)} %broadcast_add_fusion.16, ...), kind=kLoop, calls=%fused_computation.136.clone.1 | loop fusion | flops 15727872 | bytes 1282080 | tf_op jit(solution)/shard_map/while/body/eval_jaxpr/reduce_sum | solution.py:172
  324.4 4.0 %fusion.574 = (f32[16,128]{1,0:T(8,128)S(1)}, f32[16,128]{1,0:T(8,128)S(1)}, f32[16,128]{1,0:T(8,128)S(1)}) fusion(f32[16,128]{1,0:T(8,128)S(1)} %bitcast.711, f32[16,128]{1,0:T(8,128)S(1)} %bitcast.791, f32[16,128]{1,0:T(8,128)S(1)} %bitcast.943, f32[16,128]{1,0:T(8,128)S(1)} %bitcast.713, f32[16,128]{1,0:T(8,128)S(1)} %bitcast.712, ...), kind=kLoop, calls=%fused_computation.759 | loop fusion | flops 15460352 | bytes 131088 | tf_op jit(solution)/shard_map/reduce_sum | solution.py:79
  332.4 4.0 %fusion.610 = (f32[16,128]{1,0:T(8,128)S(1)}, f32[16,128]{1,0:T(8,128)S(1)}, f32[16,128]{1,0:T(8,128)S(1)}) fusion(f32[16,128]{1,0:T(8,128)S(1)} %bitcast.879, f32[16,128]{1,0:T(8,128)S(1)} %bitcast.764, f32[16,128]{1,0:T(8,128)S(1)} %bitcast.945, f32[16,128]{1,0:T(8,128)S(1)} %bitcast.881, f32[16,128]{1,0:T(8,128)S(1)} %bitcast.880, ...), kind=kLoop, calls=%fused_computation.795 | loop fusion | flops 15460352 | bytes 131088 | tf_op jit(solution)/shard_map/reduce_sum | solution.py:79
  340.4 7.3 %fusion.628 = (f32[16,128]{1,0:T(8,128)S(1)}, f32[16,128]{1,0:T(8,128)S(1)}, f32[16,128]{1,0:T(8,128)S(1)}, f32[16,128]{1,0:T(8,128)S(1)}, f32[16,128]{1,0:T(8,128)S(1)}, /*index=5*/f32[16,128]{1,0:T(8,128)S(1)}) fusion(f32[16,128]{1,0:T(8,128)S(1)} %bitcast.862, f32[16,128]{1,0:T(8,128)S(1)} %bitcast.737, f32[16,128]{1,0:T(8,128)S(1)} %bitcast.947, ...), kind=kLoop, calls=%fused_computation.813 | loop fusion | flops 30920704 | bytes 180256 | tf_op jit(solution)/shard_map/reduce_sum | solution.py:79
  349.4 31.7 %psum.79 = f32[]{:T(128)} all-reduce(f32[]{:T(128)} %get-tuple-element.1104), channel_id=1, replica_groups=mesh['groups'=2,'blk'=4,'oct'=2,'sub'=2] {'blk','oct','sub'}, use_global_device_ids=true, to_apply=%region_112.113 | all-reduce | flops 1 | bytes 8 | tf_op jit(solution)/shard_map/psum | solution.py:231
  (193 shorter events, 96.8 us)
Async XLA Ops:
  0.6 30.1 %copy-start.8 = (f32[5,5,1]{1,0,2:T(8,128)S(1)}, f32[5,5,1]{1,0,2:T(8,128)}, u32[]{:S(2)}) copy-start(f32[5,5,1]{1,0,2:T(8,128)} %constant.532) | copy-start | bytes 304
  0.6 30.3 %copy-start.11 = (f32[128,5,1]{0,1,2:T(8,128)S(1)}, f32[128,5,1]{0,1,2:T(8,128)}, u32[]{:S(2)}) copy-start(f32[128,5,1]{0,1,2:T(8,128)} %constant.533) | copy-start | bytes 7684
  2.1 67.6 %collective-permute-start = (f32[5,512]{1,0:T(8,128)S(1)}, f32[5,512]{1,0:T(8,128)S(1)}, u32[]{:S(2)}, u32[]{:S(2)}) collective-permute-start(f32[5,512]{1,0:T(8,128)S(1)} %get-tuple-element.989), channel_id=1, source_target_pairs={{0,1},{1,2},{2,3},{3,4},{4,5},{5,6},{6,7},{7,8},{8,9},{9,10},{10,1... | collective-permute-start | bytes 30728 | tf_op jit(solution)/shard_map/ppermute | solution.py:35
  2.6 67.1 %collective-permute-start.2 = (f32[5,512]{1,0:T(8,128)S(1)}, f32[5,512]{1,0:T(8,128)S(1)}, u32[]{:S(2)}, u32[]{:S(2)}) collective-permute-start(f32[5,512]{1,0:T(8,128)S(1)} %get-tuple-element.990), channel_id=1, source_target_pairs={{1,0},{2,1},{3,2},{4,3},{5,4},{6,5},{7,6},{8,7},{9,8},{10,9},{11,1... | collective-permute-start | bytes 30728 | tf_op jit(solution)/shard_map/ppermute | solution.py:37
  8.6 61.0 %collective-permute-start.1 = (f32[3,512]{1,0:T(4,128)S(1)}, f32[3,512]{1,0:T(4,128)S(1)}, u32[]{:S(2)}, u32[]{:S(2)}) collective-permute-start(f32[3,512]{1,0:T(4,128)S(1)} %get-tuple-element.1085), channel_id=1, source_target_pairs={{0,1},{1,2},{2,3},{3,4},{4,5},{5,6},{6,7},{7,8},{8,9},{9,10},{10,1... | collective-permute-start | bytes 18440 | tf_op jit(solution)/shard_map/ppermute | solution.py:35
  8.6 61.0 %collective-permute-start.3 = (f32[3,512]{1,0:T(4,128)S(1)}, f32[3,512]{1,0:T(4,128)S(1)}, u32[]{:S(2)}, u32[]{:S(2)}) collective-permute-start(f32[3,512]{1,0:T(4,128)S(1)} %get-tuple-element.1086), channel_id=1, source_target_pairs={{1,0},{2,1},{3,2},{4,3},{5,4},{6,5},{7,6},{8,7},{9,8},{10,9},{11,1... | collective-permute-start | bytes 18440 | tf_op jit(solution)/shard_map/ppermute | solution.py:37
  13.1 19.8 %copy-start.10 = (f32[128,5,1]{0,1,2:T(8,128)S(1)}, f32[128,5,1]{0,1,2:T(8,128)}, u32[]{:S(2)}) copy-start(f32[128,5,1]{0,1,2:T(8,128)} %constant.534) | copy-start | bytes 7684
  32.8 1.8 copy-start.9
  36.5 19.2 %copy-start.2 = (f32[128]{0:T(128)S(1)}, f32[128]{0:T(128)}, u32[]{:S(2)}) copy-start(f32[128]{0:T(128)} %constant.2011) | copy-start | bytes 1540
  36.5 19.2 %copy-start.4 = (f32[128]{0:T(128)S(1)}, f32[128]{0:T(128)}, u32[]{:S(2)}) copy-start(f32[128]{0:T(128)} %constant.489.clone..sunk.15) | copy-start | bytes 1540
  36.5 19.2 %copy-start.5 = (f32[128]{0:T(128)S(1)}, f32[128]{0:T(128)}, u32[]{:S(2)}) copy-start(f32[128]{0:T(128)} %constant.2010) | copy-start | bytes 1540
  36.5 19.2 %copy-start.6 = (f32[128]{0:T(128)S(1)}, f32[128]{0:T(128)}, u32[]{:S(2)}) copy-start(f32[128]{0:T(128)} %constant.490.clone..sunk.15) | copy-start | bytes 1540
  36.5 19.2 %copy-start.7 = (f32[128]{0:T(128)S(1)}, f32[128]{0:T(128)}, u32[]{:S(2)}) copy-start(f32[128]{0:T(128)} %constant.2009) | copy-start | bytes 1540
  55.7 13.5 %copy-start = (s32[16,9]{1,0:T(8,128)S(1)}, s32[16,9]{1,0:T(8,128)}, u32[]{:S(2)}) copy-start(s32[16,9]{1,0:T(8,128)} %param.28) | copy-start | bytes 1732
  55.7 13.8 %copy-start.1 = (f32[2048]{0:T(1024)S(1)}, f32[2048]{0:T(1024)}, u32[]{:S(2)}) copy-start(f32[2048]{0:T(1024)} %param.25) | copy-start | bytes 24580
  55.7 14.0 %copy-start.3 = (f32[3,2048]{1,0:T(4,128)S(1)}, f32[3,2048]{1,0:T(4,128)}, u32[]{:S(2)}) copy-start(f32[3,2048]{1,0:T(4,128)} %param.24) | copy-start | bytes 73732
  123.3 35.3 %collective-permute-start.4 = (f32[3,512]{1,0:T(4,128)S(1)}, f32[3,512]{1,0:T(4,128)S(1)}, u32[]{:S(2)}, u32[]{:S(2)}) collective-permute-start(f32[3,512]{1,0:T(4,128)S(1)} %get-tuple-element.1077), channel_id=1, source_target_pairs={{0,1},{1,2},{2,3},{3,4},{4,5},{5,6},{6,7},{7,8},{8,9},{9,10},{10,1... | collective-permute-start | bytes 18440 | tf_op jit(solution)/shard_map/ppermute | solution.py:35
  123.3 35.2 %collective-permute-start.5 = (f32[3,512]{1,0:T(4,128)S(1)}, f32[3,512]{1,0:T(4,128)S(1)}, u32[]{:S(2)}, u32[]{:S(2)}) collective-permute-start(f32[3,512]{1,0:T(4,128)S(1)} %get-tuple-element.1078), channel_id=1, source_target_pairs={{1,0},{2,1},{3,2},{4,3},{5,4},{6,5},{7,6},{8,7},{9,8},{10,9},{11,1... | collective-permute-start | bytes 18440 | tf_op jit(solution)/shard_map/ppermute | solution.py:37
  276.6 35.6 %collective-permute-start.6 = (f32[3,512]{1,0:T(4,128)S(1)}, f32[3,512]{1,0:T(4,128)S(1)}, u32[]{:S(2)}, u32[]{:S(2)}) collective-permute-start(f32[3,512]{1,0:T(4,128)S(1)} %get-tuple-element.1069), channel_id=1, source_target_pairs={{0,1},{1,2},{2,3},{3,4},{4,5},{5,6},{6,7},{7,8},{8,9},{9,10},{10,1... | collective-permute-start | bytes 18440 | tf_op jit(solution)/shard_map/ppermute | solution.py:35
  276.7 35.6 %collective-permute-start.7 = (f32[3,512]{1,0:T(4,128)S(1)}, f32[3,512]{1,0:T(4,128)S(1)}, u32[]{:S(2)}, u32[]{:S(2)}) collective-permute-start(f32[3,512]{1,0:T(4,128)S(1)} %get-tuple-element.1070), channel_id=1, source_target_pairs={{1,0},{2,1},{3,2},{4,3},{5,4},{6,5},{7,6},{8,7},{9,8},{10,9},{11,1... | collective-permute-start | bytes 18440 | tf_op jit(solution)/shard_map/ppermute | solution.py:37
